TPU v7x, 512 devices: a whole 4x8x8 slice. The times are simulated.
512 devices in a mesh: tp: 64 (over y, z_hi, core), ep: 8 (over x, z_lo).
Axes of the slice: x: 4, y: 8, z: 8 (z_hi: 4, z_lo: 2; z = z_hi * 2 + z_lo), core: 2. Of those that a mesh axis runs over, the one named last changes fastest.
Arguments:
- residual: bfloat16 [8, 7168, 256], P('ep', 'tp')
- out_grad: bfloat16 [8, 7168, 256], P('ep', 'tp'), may hold values from -6 to 6
- norm_gain: float32 [7168], P('tp'), may hold values from 0.25 to 1.75
- context: bfloat16 [8, 16384, 256], P('ep', 'tp'), may hold values from -0.3125 to 0.3125
- w_out: bfloat16 [7168, 16384], P('ep', 'tp'), may hold values from -0.046875 to 0.046875
- w_gate: bfloat16 [8, 7168, 2048], P('ep', 'tp'), may hold values from -0.0625 to 0.0625
- w_up: bfloat16 [8, 7168, 2048], P('ep', 'tp'), may hold values from -0.0625 to 0.0625
- w_down: bfloat16 [8, 7168, 2048], P('ep', 'tp'), may hold values from -0.125 to 0.125
- slot_token: int32 [8, 8, 8], P('ep'), may hold values from 0 to 255, as said below
- slot_count: int32 [8, 8], P('ep'), may hold values from 1 to 8, as said below
- slot_gate: float32 [8, 8, 8], P('ep'), may hold values from 0.25 to 2.5
Outputs:
- resid_grad: bfloat16 [8, 7168, 256], P('ep', 'tp')
- context_grad: bfloat16 [8, 16384, 256], P('ep', 'tp')
- w_out_grad: bfloat16 [7168, 16384], P('ep', 'tp')
- gate_grad: bfloat16 [8, 7168, 2048], P('ep', 'tp')
- up_grad: bfloat16 [8, 7168, 2048], P('ep', 'tp')
- down_grad: bfloat16 [8, 7168, 2048], P('ep', 'tp')
Inputs may be any that keep to these rules, and one draw needn't show every extreme that they name: `slot_token`: within one group and expert the 8 token positions are distinct; slots at or beyond slot_count are unused. `slot_count`: in every draw one expert has 8 tokens from every group.
All inputs are finite; a program needn't handle non-finite values.
Results may differ from a plain program's by a relative error of at most 0.014.
Values may be sent and summed in bfloat16 or wider, within the bound.
A program may use at most 64 MiB of HBM per device.

v0:
```python
import jax
import jax.numpy as jnp
from jax import lax
from jax.sharding import PartitionSpec as P

norm_eps = 1e-06


def contract_rows(left, right):
    return lax.dot_general(
        left, right, (((0,), (0,)), ((), ())), preferred_element_type=jnp.float32
    )


def contract_cols(left, right):
    return lax.dot_general(
        left, right, (((1,), (1,)), ((), ())), preferred_element_type=jnp.float32
    )


def activate(pre_gate, pre_up, hid_grad):
    sigmoid_gate = jax.nn.sigmoid(pre_gate)
    silu_gate = pre_gate * sigmoid_gate
    hidden = (silu_gate * pre_up).astype(jnp.bfloat16)
    d_gate = (hid_grad * pre_up * sigmoid_gate * (1.0 + pre_gate * (1.0 - sigmoid_gate))).astype(
        jnp.bfloat16
    )
    d_up = (hid_grad * silu_gate).astype(jnp.bfloat16)
    return (hidden, d_gate, d_up)


def shards(
    residual,
    out_grad,
    norm_gain,
    context,
    w_out,
    w_gate,
    w_up,
    w_down,
    slot_token,
    slot_count,
    slot_gate,
):
    tp_count = lax.axis_size("tp")
    stream = residual[0].astype(jnp.float32)
    grad_in = out_grad[0].astype(jnp.float32)
    feat_share, group_rows = stream.shape
    features = feat_share * tp_count
    square = lax.psum(jnp.sum(stream * stream, axis=0), "tp")
    inv_rms = lax.rsqrt(square / features + norm_eps)[None, :]
    normed = stream * inv_rms
    gain_col = norm_gain[:, None]
    inputs = (normed * gain_col).astype(jnp.bfloat16)
    slot_table = slot_token[0]
    capacity = slot_table.shape[1]
    live_mask = jnp.arange(capacity)[None, :] < slot_count[0][:, None]
    one_hot = (
        (slot_table[:, :, None] == jnp.arange(group_rows)[None, None, :]) & live_mask[:, :, None]
    ).astype(jnp.bfloat16)
    send_x = jnp.einsum("dt,ect->edc", inputs, one_hot, preferred_element_type=jnp.float32).astype(
        jnp.bfloat16
    )
    go_rows = jnp.einsum("dt,ect->edc", out_grad[0], one_hot, preferred_element_type=jnp.float32)
    send_go = (slot_gate[0][:, None, :] * go_rows).astype(jnp.bfloat16)
    recv_x, recv_go = (
        lax.all_to_all(send_x, "ep", split_axis=0, concat_axis=2, tiled=True),
        lax.all_to_all(send_go, "ep", split_axis=0, concat_axis=2, tiled=True),
    )
    rows_x = recv_x[0]
    rows_go = recv_go[0]
    gate_w = w_gate[0]
    up_w = w_up[0]
    down_w = w_down[0]
    gate_part = contract_rows(rows_x, gate_w)
    up_part = contract_rows(rows_x, up_w)
    hid_part = contract_rows(rows_go, down_w)
    pre_gate, pre_up, hid_grad = lax.psum((gate_part, up_part, hid_part), "tp")
    hidden, d_gate, d_up = activate(pre_gate, pre_up, hid_grad)
    down_grad = jnp.dot(rows_go, hidden, preferred_element_type=jnp.float32).astype(jnp.bfloat16)[
        None
    ]
    gate_grad = jnp.dot(rows_x, d_gate, preferred_element_type=jnp.float32).astype(jnp.bfloat16)[
        None
    ]
    up_grad = jnp.dot(rows_x, d_up, preferred_element_type=jnp.float32).astype(jnp.bfloat16)[None]
    slot_back = (contract_cols(gate_w, d_gate) + contract_cols(up_w, d_up)).astype(jnp.bfloat16)
    returned = lax.all_to_all(slot_back[None], "ep", split_axis=2, concat_axis=0, tiled=True)
    in_grad = jnp.einsum(
        "edc,ect->dt", returned, one_hot, preferred_element_type=jnp.float32
    ).astype(jnp.bfloat16)
    scaled = in_grad.astype(jnp.float32) * gain_col
    dots = lax.psum(jnp.sum(scaled * normed, axis=0), "tp")
    resid = (grad_in + inv_rms * (scaled - normed * (dots / features)[None, :])).astype(
        jnp.bfloat16
    )
    full_grad = lax.all_gather(resid, "tp", axis=0, tiled=True)
    grad_block = lax.all_to_all(full_grad, "ep", split_axis=0, concat_axis=1, tiled=True)
    ctx_local = context[0]
    ctx_all = lax.all_gather(ctx_local, "ep", axis=1, tiled=True)
    weight_sum = contract_cols(grad_block, ctx_all)
    ctx_total = contract_rows(lax.all_gather(w_out, "ep", axis=0, tiled=True), full_grad)
    return (
        resid[None],
        ctx_total.astype(jnp.bfloat16)[None],
        weight_sum.astype(jnp.bfloat16),
        gate_grad,
        up_grad,
        down_grad,
    )


def solution(mesh):
    return jax.shard_map(
        shards,
        mesh=mesh,
        in_specs=(
            P("ep", "tp", None),
            P("ep", "tp", None),
            P("tp"),
            P("ep", "tp", None),
            P("ep", "tp"),
            P("ep", "tp", None),
            P("ep", "tp", None),
            P("ep", "tp", None),
            P("ep", None, None),
            P("ep", None),
            P("ep", None, None),
        ),
        out_specs=(
            P("ep", "tp", None),
            P("ep", "tp", None),
            P("ep", "tp"),
            P("ep", "tp", None),
            P("ep", "tp", None),
            P("ep", "tp", None),
        ),
        check_vma=False,
    )
```

profile of v0, /device:TPU:2, one launch (start us, length us, event | category | flops | bytes accessed | tf_op | source)
XLA Modules:
  0.0 1152.4 jit_solution(9309882180991946875)
XLA Ops:
  7.2 0.0 copy-start
  7.2 0.9 fusion.32
  8.1 150.2 %psum.35 = f32[256]{0:T(256)S(1)} all-reduce(f32[256]{0:T(256)S(1)} %fusion.32), channel_id=1, replica_groups=mesh['tp'=64,'ep'=8] {'tp'}, use_global_device_ids=true, to_apply=%region_1.0 | all-reduce | flops 256 | bytes 2048 | tf_op jit(solution)/shard_map/psum | solution.py:50
  158.3 0.7 iota_compare_fusion.1
  159.1 1.6 fusion.9
  160.7 5.7 all-to-all-start.1
  166.5 1.6 fusion.11
  168.1 3.1 all-to-all-done.1
  171.2 4.7 all-to-all-start
  175.9 0.0 all-reduce.3.cloned.1.call-start
  175.9 0.0 copy-done
  175.9 1.0 fusion.16
  177.0 2.1 fusion.19
  179.1 1.7 all-to-all-done
  180.7 2.0 fusion.21
  182.8 0.0 all-reduce.3.cloned.1.call-update
  182.8 0.0 all-gather.5.cloned.1.call-start
  182.8 554.5 %all-reduce.3.cloned.1.call-done = (f32[64,2048]{1,0:T(8,128)}, f32[64,2048]{1,0:T(8,128)}, f32[64,2048]{1,0:T(8,128)}) async-done(((f32[64,2048]{1,0:T(8,128)}, f32[64,2048]{1,0:T(8,128)}, f32[64,2048]{1,0:T(8,128)}), (f32[64,2048]{1,0:T(8,128)}, f32[64,2048]{1,0:T(8,128)}, f32[64,2048]{1,0:T(8,128)})) %all-reduce.3.cloned.1.call-update) | async-done | bytes 1572880 | tf_op jit(solution)/shard_map/psum | solution.py:78
  737.3 1.6 multiply_convert_fusion.1
  738.9 0.3 fusion.14
  739.2 0.0 copy-done.1
  739.3 0.3 fusion.10
  739.6 0.5 broadcast.36
  740.1 0.7 reduce
  740.8 0.1 reshape.53
  740.9 9.5 all_to_all.67
  750.5 0.1 reshape.54
  750.6 0.0 copy-done.4
  750.6 0.3 fusion.27
  750.9 142.3 %psum.39 = f32[256]{0:T(256)S(1)} all-reduce(f32[256]{0:T(256)S(1)} %get-tuple-element.35), channel_id=1, replica_groups=mesh['tp'=64,'ep'=8] {'tp'}, use_global_device_ids=true, to_apply=%region_6.0 | all-reduce | flops 256 | bytes 2048 | tf_op jit(solution)/shard_map/psum | solution.py:93
  893.2 0.7 fusion.31
  893.9 0.0 all-gather.5.cloned.1.call-update
  893.9 0.0 all-gather.7.cloned.1.call-start
  893.9 0.7 all-gather.7.cloned.1.call-update
  894.6 78.9 %all-gather.5.cloned.1.call-done = bf16[7168,256]{1,0:T(8,128)(2,1)} async-done(((bf16[112,256]{1,0:T(8,128)(2,1)}), bf16[7168,256]{1,0:T(8,128)(2,1)}) %all-gather.5.cloned.1.call-update) | async-done | bytes 3670032 | tf_op jit(solution)/shard_map/all_gather | solution.py:97
  973.5 6.2 copy.32
  979.8 6.5 all-to-all-start.3
  986.3 0.6 all-gather.9.cloned.1.call-update
  986.9 1.1 fusion
  987.9 1.1 fusion.1
  989.0 0.0 copy-done.3
  989.0 1.1 fusion.2
  990.1 107.2 %all-gather.7.cloned.1.call-done = bf16[7168,256]{1,0:T(8,128)(2,1)} async-done(((bf16[896,256]{1,0:T(8,128)(2,1)}), bf16[7168,256]{1,0:T(8,128)(2,1)}) %all-gather.7.cloned.1.call-update) | async-done | bytes 3670032 | tf_op jit(solution)/shard_map/all_gather | solution.py:102
  1097.3 4.3 fusion.3
  1101.6 0.8 copy.33
  1102.4 39.3 %all-gather.9.cloned.1.call-done = bf16[1,256,2048]{2,1,0:T(8,128)(2,1)} async-done(((bf16[1,256,256]{2,1,0:T(8,128)(2,1)}), bf16[1,256,2048]{2,1,0:T(8,128)(2,1)}) %all-gather.9.cloned.1.call-update) | async-done | bytes 1048592 | tf_op jit(solution)/shard_map/all_gather | solution.py:100
  1141.6 0.0 all-to-all-done.3
  1141.6 4.3 convolution_convert_fusion.3
  (15 shorter events, 0.1 us)
Async XLA Ops:
  7.2 168.8 %copy-start = (bf16[1,112,2048]{2,1,0:T(8,128)(2,1)S(1)}, bf16[1,112,2048]{2,1,0:T(8,128)(2,1)}, u32[]{:S(2)}) copy-start(bf16[1,112,2048]{2,1,0:T(8,128)(2,1)} %param.16) | copy-start | bytes 1376260
  160.7 10.5 all-to-all-start.1
  171.2 9.5 all-to-all-start
  175.9 563.3 %copy-start.1 = (bf16[1,112,2048]{2,1,0:T(8,128)(2,1)S(1)}, bf16[1,112,2048]{2,1,0:T(8,128)(2,1)}, u32[]{:S(2)}) copy-start(bf16[1,112,2048]{2,1,0:T(8,128)(2,1)} %param.17) | copy-start | bytes 1376260
  175.9 561.4 %all-reduce.3.cloned.1.call-start = ((), (), s32[]{:S(2)}) async-start(), calls=%async_computation.7 | async-start | bytes 3145728 | tf_op jit(solution)/shard_map/psum | solution.py:78
  176.9 573.6 %copy-start.4 = (bf16[1,112,256]{2,1,0:T(8,128)(2,1)S(1)}, bf16[1,112,256]{2,1,0:T(8,128)(2,1)}, u32[]{:S(2)}) copy-start(bf16[1,112,256]{2,1,0:T(8,128)(2,1)} %param.11) | copy-start | bytes 172036
  176.9 573.6 %copy-start.6 = (s32[1,8,8]{2,1,0:T(8,128)S(1)}, s32[1,8,8]{2,1,0:T(8,128)}, u32[]{:S(2)}) copy-start(s32[1,8,8]{2,1,0:T(8,128)} %param.19) | copy-start | bytes 772
  177.0 573.6 %copy-start.7 = (f32[112]{0:T(128)S(1)}, f32[112]{0:T(128)}, u32[]{:S(2)}) copy-start(f32[112]{0:T(128)} %param.13) | copy-start | bytes 1348
  177.0 716.3 %copy-start.5 = (bf16[1,112,256]{2,1,0:T(8,128)(2,1)S(1)}, bf16[1,112,256]{2,1,0:T(8,128)(2,1)}, u32[]{:S(2)}) copy-start(bf16[1,112,256]{2,1,0:T(8,128)(2,1)} %param.12) | copy-start | bytes 172036
  182.8 790.7 %all-gather.5.cloned.1.call-start = ((), (), s32[]{:S(2)}) async-start(), calls=%async_computation.4 | async-start | bytes 3727360 | tf_op jit(solution)/shard_map/all_gather | solution.py:97
  893.9 203.4 %all-gather.7.cloned.1.call-start = ((), (), s32[]{:S(2)}) async-start(), calls=%async_computation.5 | async-start | bytes 4128768 | tf_op jit(solution)/shard_map/all_gather | solution.py:102
  979.8 9.3 copy-start.2
  979.8 9.3 copy-start.3
  979.8 161.9 %all-to-all-start.3 = ((bf16[8,896,256]{1,2,0:T(8,128)(2,1)}), bf16[8,896,256]{1,2,0:T(8,128)(2,1)}, u32[]{:S(2)}, u32[]{:S(2)}) async-start(bf16[8,896,256]{1,2,0:T(8,128)(2,1)} %copy.32), calls=%async_computation.3 | async-start | bytes 7340032 | tf_op jit(solution)/shard_map/all_to_all | solution.py:98
  986.3 155.3 %all-gather.9.cloned.1.call-start = ((), (), s32[]{:S(2)}) async-start(), calls=%async_computation.6 | async-start | bytes 1179648 | tf_op jit(solution)/shard_map/all_gather | solution.py:100
Sparse Core Ops, SparseCore 0:
  182.9 554.3 all-reduce.2
  894.0 79.4 all-gather.4
  975.8 121.4 all-gather.6
  1099.3 42.2 all-gather.8
where the time goes:
time: 1150 us
  waiting for transfers between devices  786 us (68%)
  blocking collectives  302 us (26%)
  matrix products  21.1 us (2%)
  starting transfers between devices  17.1 us (1%)
  between operations  13.9 us (1%)
    psum x1, waiting for transfers between devices, shards(): pre_gate, pre_up, hid_grad = lax.psum((gate_part, up_part, hid_part), 'tp')  555 us
    psum x1, blocking collectives, shards(): square = lax.psum(jnp.sum(stream * stream, axis=0), 'tp')  150 us
    psum x1, blocking collectives, shards(): dots = lax.psum(jnp.sum(scaled * normed, axis=0), 'tp')  142 us
    all_gather x1, waiting for transfers between devices, shards(): lax.all_gather(w_out, 'ep', axis=0, tiled=True)  107 us
    all_gather x1, waiting for transfers between devices, shards(): full_grad = lax.all_gather(resid, 'tp', axis=0, tiled=True)  78.9 us
    all_gather x1, waiting for transfers between devices, shards(): ctx_all = lax.all_gather(ctx_local, 'ep', axis=1, tiled=True)  39.3 us
  transfers between devices with their start and end apart: 7, of which 6 were waited for; matrix products, arithmetic and copies ran while one was open for 2% of the time, Pallas kernels for 0%

commit v1 on v0

--- a/solution.py
+++ b/solution.py
@@ -90,7 +90,7 @@
         "edc,ect->dt", returned, one_hot, preferred_element_type=jnp.float32
     ).astype(jnp.bfloat16)
     scaled = in_grad.astype(jnp.float32) * gain_col
-    dots = lax.psum(jnp.sum(scaled * normed, axis=0), "tp")
+    dots = jnp.sum(lax.all_gather(jnp.sum(scaled * normed, axis=0), "tp"), axis=0)
     resid = (grad_in + inv_rms * (scaled - normed * (dots / features)[None, :])).astype(
         jnp.bfloat16
     )

time: 1150 us -> 1090 us (0.948)
  blocking collectives: 302 us -> 240 us
    psum x1 -> x0, blocking collectives: 142 us -> none  [shards(): dots = lax.psum(jnp.sum(scaled * normed, axis=0), 'tp')]
    all_gather x0 -> x1, blocking collectives: none -> 80.4 us  [shards(): lax.all_gather(jnp.sum(scaled * normed, axis=0), 'tp')]
where the time goes in v1:
time: 1090 us
  waiting for transfers between devices  786 us (72%)
  blocking collectives  240 us (22%)
  matrix products  21.1 us (2%)
  starting transfers between devices  17.1 us (2%)
  between operations  13.9 us (1%)
    psum x1, waiting for transfers between devices, shards(): pre_gate, pre_up, hid_grad = lax.psum((gate_part, up_part, hid_part), 'tp')  555 us
    psum x1, blocking collectives, shards(): square = lax.psum(jnp.sum(stream * stream, axis=0), 'tp')  150 us
    all_gather x1, waiting for transfers between devices, shards(): lax.all_gather(w_out, 'ep', axis=0, tiled=True)  107 us
    all_gather x1, blocking collectives, shards(): lax.all_gather(jnp.sum(scaled * normed, axis=0), 'tp')  80.4 us
    all_gather x1, waiting for transfers between devices, shards(): full_grad = lax.all_gather(resid, 'tp', axis=0, tiled=True)  78.7 us
    all_gather x1, waiting for transfers between devices, shards(): ctx_all = lax.all_gather(ctx_local, 'ep', axis=1, tiled=True)  39.3 us
  transfers between devices with their start and end apart: 7, of which 6 were waited for; matrix products, arithmetic and copies ran while one was open for 2% of the time, Pallas kernels for 0%

profile of v1, /device:TPU:2, one launch (start us, length us, event | category | flops | bytes accessed | tf_op | source)
XLA Modules:
  0.0 1090.3 jit_solution(11343329542706530227)
XLA Ops:
  7.2 0.0 copy-start
  7.2 0.9 fusion.32
  8.1 150.2 %psum.28 = f32[256]{0:T(256)S(1)} all-reduce(f32[256]{0:T(256)S(1)} %fusion.32), channel_id=1, replica_groups=mesh['tp'=64,'ep'=8] {'tp'}, use_global_device_ids=true, to_apply=%region_1.0 | all-reduce | flops 256 | bytes 2048 | tf_op jit(solution)/shard_map/psum | solution.py:50
  158.3 0.7 iota_compare_fusion.1
  159.1 1.6 fusion.9
  160.7 5.7 all-to-all-start.1
  166.5 1.6 fusion.11
  168.1 3.1 all-to-all-done.1
  171.2 4.7 all-to-all-start
  175.9 0.0 all-reduce.3.cloned.1.call-start
  175.9 0.0 copy-done
  175.9 1.0 fusion.16
  177.0 2.1 fusion.19
  179.1 1.7 all-to-all-done
  180.7 2.0 fusion.21
  182.8 0.0 all-reduce.3.cloned.1.call-update
  182.8 0.0 all-gather.7.cloned.1.call-start
  182.8 554.5 %all-reduce.3.cloned.1.call-done = (f32[64,2048]{1,0:T(8,128)}, f32[64,2048]{1,0:T(8,128)}, f32[64,2048]{1,0:T(8,128)}) async-done(((f32[64,2048]{1,0:T(8,128)}, f32[64,2048]{1,0:T(8,128)}, f32[64,2048]{1,0:T(8,128)}), (f32[64,2048]{1,0:T(8,128)}, f32[64,2048]{1,0:T(8,128)}, f32[64,2048]{1,0:T(8,128)})) %all-reduce.3.cloned.1.call-update) | async-done | bytes 1572880 | tf_op jit(solution)/shard_map/psum | solution.py:78
  737.3 1.6 multiply_convert_fusion.1
  738.9 0.3 fusion.14
  739.3 0.3 fusion.10
  739.6 0.5 broadcast.39
  740.1 0.7 reduce.1
  740.8 0.1 reshape.59
  740.9 9.5 all_to_all.67
  750.5 0.1 reshape.60
  750.6 0.3 fusion.27
  750.9 80.4 %all-gather.2 = f32[64,1,256]{2,1,0:T(1,128)S(1)} all-gather(f32[1,1,256]{2,1,0:T(1,128)S(1)} %bitcast.114), channel_id=2, replica_groups=mesh['tp'=64,'ep'=8] {'tp'}, dimensions={0}, use_global_device_ids=true | all-gather | bytes 66560 | tf_op jit(solution)/shard_map/all_gather | solution.py:93
  831.3 0.1 reduce_sum.29
  831.4 0.0 copy-done.5
  831.4 0.7 fusion.31
  832.0 0.0 all-gather.7.cloned.1.call-update
  832.0 0.0 all-gather.9.cloned.1.call-start
  832.1 0.7 all-gather.9.cloned.1.call-update
  832.8 78.7 %all-gather.7.cloned.1.call-done = bf16[7168,256]{1,0:T(8,128)(2,1)} async-done(((bf16[112,256]{1,0:T(8,128)(2,1)}), bf16[7168,256]{1,0:T(8,128)(2,1)}) %all-gather.7.cloned.1.call-update) | async-done | bytes 3670032 | tf_op jit(solution)/shard_map/all_gather | solution.py:97
  911.4 6.2 copy.32
  917.7 6.5 all-to-all-start.3
  924.2 0.6 all-gather.11.cloned.1.call-update
  924.8 1.1 fusion
  925.9 1.1 fusion.1
  926.9 0.0 copy-done.3
  926.9 1.1 fusion.2
  928.0 107.2 %all-gather.9.cloned.1.call-done = bf16[7168,256]{1,0:T(8,128)(2,1)} async-done(((bf16[896,256]{1,0:T(8,128)(2,1)}), bf16[7168,256]{1,0:T(8,128)(2,1)}) %all-gather.9.cloned.1.call-update) | async-done | bytes 3670032 | tf_op jit(solution)/shard_map/all_gather | solution.py:102
  1035.2 4.3 fusion.3
  1039.5 0.8 copy.33
  1040.3 39.3 %all-gather.11.cloned.1.call-done = bf16[1,256,2048]{2,1,0:T(8,128)(2,1)} async-done(((bf16[1,256,256]{2,1,0:T(8,128)(2,1)}), bf16[1,256,2048]{2,1,0:T(8,128)(2,1)}) %all-gather.11.cloned.1.call-update) | async-done | bytes 1048592 | tf_op jit(solution)/shard_map/all_gather | solution.py:100
  1079.5 0.0 all-to-all-done.3
  1079.6 4.3 convolution_convert_fusion.3
  (16 shorter events, 0.1 us)
Async XLA Ops:
  7.2 168.8 %copy-start = (bf16[1,112,2048]{2,1,0:T(8,128)(2,1)S(1)}, bf16[1,112,2048]{2,1,0:T(8,128)(2,1)}, u32[]{:S(2)}) copy-start(bf16[1,112,2048]{2,1,0:T(8,128)(2,1)} %param.16) | copy-start | bytes 1376260
  160.7 10.5 all-to-all-start.1
  171.2 9.5 all-to-all-start
  175.9 563.3 %copy-start.1 = (bf16[1,112,2048]{2,1,0:T(8,128)(2,1)S(1)}, bf16[1,112,2048]{2,1,0:T(8,128)(2,1)}, u32[]{:S(2)}) copy-start(bf16[1,112,2048]{2,1,0:T(8,128)(2,1)} %param.17) | copy-start | bytes 1376260
  175.9 561.4 %all-reduce.3.cloned.1.call-start = ((), (), s32[]{:S(2)}) async-start(), calls=%async_computation.7 | async-start | bytes 3145728 | tf_op jit(solution)/shard_map/psum | solution.py:78
  176.9 573.6 %copy-start.4 = (bf16[1,112,256]{2,1,0:T(8,128)(2,1)S(1)}, bf16[1,112,256]{2,1,0:T(8,128)(2,1)}, u32[]{:S(2)}) copy-start(bf16[1,112,256]{2,1,0:T(8,128)(2,1)} %param.11) | copy-start | bytes 172036
  176.9 573.6 %copy-start.6 = (s32[1,8,8]{2,1,0:T(8,128)S(1)}, s32[1,8,8]{2,1,0:T(8,128)}, u32[]{:S(2)}) copy-start(s32[1,8,8]{2,1,0:T(8,128)} %param.19) | copy-start | bytes 772
  177.0 573.6 %copy-start.7 = (f32[112]{0:T(128)S(1)}, f32[112]{0:T(128)}, u32[]{:S(2)}) copy-start(f32[112]{0:T(128)} %param.13) | copy-start | bytes 1348
  177.0 654.4 %copy-start.5 = (bf16[1,112,256]{2,1,0:T(8,128)(2,1)S(1)}, bf16[1,112,256]{2,1,0:T(8,128)(2,1)}, u32[]{:S(2)}) copy-start(bf16[1,112,256]{2,1,0:T(8,128)(2,1)} %param.12) | copy-start | bytes 172036
  182.8 728.7 %all-gather.7.cloned.1.call-start = ((), (), s32[]{:S(2)}) async-start(), calls=%async_computation.4 | async-start | bytes 3727360 | tf_op jit(solution)/shard_map/all_gather | solution.py:97
  832.0 203.1 %all-gather.9.cloned.1.call-start = ((), (), s32[]{:S(2)}) async-start(), calls=%async_computation.5 | async-start | bytes 4128768 | tf_op jit(solution)/shard_map/all_gather | solution.py:102
  917.7 9.3 copy-start.2
  917.7 9.3 copy-start.3
  917.7 161.9 %all-to-all-start.3 = ((bf16[8,896,256]{1,2,0:T(8,128)(2,1)}), bf16[8,896,256]{1,2,0:T(8,128)(2,1)}, u32[]{:S(2)}, u32[]{:S(2)}) async-start(bf16[8,896,256]{1,2,0:T(8,128)(2,1)} %copy.32), calls=%async_computation.3 | async-start | bytes 7340032 | tf_op jit(solution)/shard_map/all_to_all | solution.py:98
  924.2 155.3 %all-gather.11.cloned.1.call-start = ((), (), s32[]{:S(2)}) async-start(), calls=%async_computation.6 | async-start | bytes 1179648 | tf_op jit(solution)/shard_map/all_gather | solution.py:100
Sparse Core Ops, SparseCore 0:
  182.9 554.3 all-reduce.2
  832.2 79.2 all-gather.6
  913.7 121.4 all-gather.8
  1037.2 42.2 all-gather.10
